TPU v7x, 32 devices: a whole 2x2x4 slice. The times are simulated.
32 devices in a mesh: lat: 2 (over x), lon: 4 (over y, core), lev: 4 (over z).
Axes of the slice: x: 2, y: 2, z: 4, core: 2. Of those that a mesh axis runs over, the one named last changes fastest.
Arguments:
- adj_final: float32 [2, 72, 32, 512], P(None, 'lev', 'lat', 'lon'), may hold values from -6 to 6
- stencil: float32 [5, 72, 32, 512], P(None, 'lev', 'lat', 'lon'), may hold values from -0.3 to 0.3
- landmask: int32 [72, 32, 512], P('lev', 'lat', 'lon'), may hold values 0 or 1
- thickness: float32 [72, 32, 512], P(None, ('lat', 'lev'), 'lon'), may hold values from 0.5 to 2
- diffusivity: float32 [72, 32, 512], P(None, ('lat', 'lev'), 'lon'), may hold values from 0.05 to 5
- level_counts: int32 [32, 512], P(('lat', 'lev'), 'lon'), may hold values from 36 to 72
- fold_partner: int32 [512], P('lon'), may hold values from 0 to 511, as said below
Outputs:
- adj_start: float32 [2, 72, 32, 512], P(None, 'lev', 'lat', 'lon')
Inputs may be any that keep to these rules, and one draw needn't show every extreme that they name: `fold_partner`: A column i in block b = i // 128 of 128 columns has its partner in block 3 - b; within a block the partners are all different.
All inputs are finite; a program needn't handle non-finite values. No bound on the sum of `landmask` on one device may be relied on, other than what follows from the above.
Results may differ from a plain program's by a relative error of at most 0.0001.
Values sent between devices are 32-bit elements; how exact they have to be, the bound alone decides.
No kernel may reach another device: no remote copies, remote signals or barrier semaphores. Data moves between devices by JAX's collectives and lax.ppermute only.
A program may use at most 64 MiB of HBM per device.

v0:
```python
import functools

import jax
import jax.numpy as jnp
from jax import lax
from jax.experimental import pallas as pl
from jax.experimental.pallas import tpu as pltpu
from jax.sharding import PartitionSpec as P


STEPS = 2
TRACERS = 2
GRANT = 12 * 2**20


def call(kernel, out_shapes, operands, scratch=(), copies=0, read_in_place=False, write_in_place=False):
    vmem, any_space = pl.BlockSpec(memory_space=pltpu.VMEM), pl.BlockSpec(memory_space=pltpu.HBM)
    return pl.pallas_call(
        kernel,
        out_shape=[jax.ShapeDtypeStruct(shape, jnp.float32) for shape in out_shapes],
        in_specs=[any_space if read_in_place else vmem] * len(operands),
        out_specs=[any_space if write_in_place else vmem] * len(out_shapes),
        scratch_shapes=[pltpu.VMEM(*shape) if isinstance(shape[0], tuple) else pltpu.VMEM(shape, jnp.float32) for shape in scratch]
        + [pltpu.SemaphoreType.DMA((copies,))] * (copies > 0),
        compiler_params=pltpu.CompilerParams(vmem_limit_bytes=GRANT),
    )(*((pltpu.with_memory_space_constraint(x, pltpu.HBM) for x in operands) if read_in_place else operands))


def span(ref, index, rows):
    return ref[pl.ds(index * rows, rows), :]


def end_values(part, levels):
    t = [part[k] for k in range(levels)]
    i = [part[levels + k] for k in range(levels + 1)]
    high, low = t[0] + i[0], jnp.ones_like(t[0])
    back_high, back_low = t[-1] + i[-1], jnp.ones_like(t[0])
    through = jnp.ones_like(t[0])
    for k in range(1, levels):
        ahead = high + i[k] * low
        high, low = t[k] * ahead + i[k] * high, ahead
        j = levels - k
        behind = back_high + i[j] * back_low
        back_high, back_low = t[j - 1] * behind + i[j] * back_high, behind
        through = through * i[k]
    scale = 1.0 / (high + i[-1] * low)
    return i[0] * back_low * scale, i[0] * through * scale, through * i[-1] * scale, i[-1] * low * scale


def pack_kernel(levels, places, thickness_ref, diffusivity_ref, counts_ref, adj_ref, *refs):
    out_refs, (near_adj_ref, held_ref, held_counts_ref, sems) = refs[:places], refs[places:]
    me = lax.axis_index("lev")
    ahead = [
        pltpu.make_async_copy(counts_ref, held_counts_ref, sems.at[0]),
        pltpu.make_async_copy(diffusivity_ref, held_ref, sems.at[1]),
    ]
    for distance in range(places):
        source = thickness_ref.at[pl.ds((me ^ distance) * levels, levels)]
        ahead.append(pltpu.make_async_copy(source, out_refs[distance].at[pl.ds(0, levels)], sems.at[2 + distance]))
    ahead.append(pltpu.make_async_copy(adj_ref, near_adj_ref, sems.at[2 + places]))
    for copy in ahead:
        copy.start()
    for copy in ahead[:2]:
        copy.wait()
    counts = held_counts_ref[...]
    last = held_ref.shape[0] - 1
    for distance in range(places):
        start = (me ^ distance) * levels
        for k in range(levels + 1):
            level = jnp.full(counts.shape, start + k, jnp.int32)
            wet = (level >= 1) & (level < counts)
            out_refs[distance][levels + k] = jnp.where(wet, held_ref[jnp.minimum(start + k, last)], 0.0)
    for copy in ahead[2:-1]:
        copy.wait()
    spikes = [end_values(out_refs[distance], levels) for distance in range(places)]
    at_end = (me >> 1) == (me & 1)
    pairs = []
    for pair in range(2):
        is_upper = (me < 2) == (pair == 0)
        one, two = spikes[2 * pair], spikes[2 * pair + 1]
        swap = at_end == (pair == 0)
        outer = [jnp.where(swap, x, y) for x, y in zip(one, two)]
        inner = [jnp.where(swap, y, x) for x, y in zip(one, two)]
        outer_near = jnp.where(is_upper, outer[3], outer[0])
        pairs.append((outer_near, *pair_factors(outer_near, inner, is_upper)))
    far_det = 1.0 / (1.0 - pairs[0][-1] * pairs[1][-1])
    for distance in range(places):
        outer_near, det, away, across, kappa, _ = pairs[distance // 2]
        far_beta = pairs[1 - distance // 2][-1]
        reach = det * across * far_det
        own = det * away + reach * far_beta * kappa
        ends_here = at_end == (distance in (0, 3))
        place = me ^ distance
        out = out_refs[distance]
        out[2 * levels + 1] = jnp.where(ends_here, own, outer_near)
        out[2 * levels + 2] = jnp.where(ends_here, reach, far_beta)
        out[levels] = jnp.where(place == 0, kappa, out[levels])
        out[2 * levels] = jnp.where(place == places - 1, kappa, out[2 * levels])
    ahead[-1].wait()


def pair_factors(outer_near, inner, is_upper):
    vf, vl, wf, wl = inner
    away, across = jnp.where(is_upper, vf, wl), jnp.where(is_upper, wf, vl)
    det = 1.0 / (1.0 - outer_near * away)
    kappa = jnp.where(is_upper, vl, wf) * det
    beta = jnp.where(is_upper, wl, vf) + kappa * outer_near * across
    return det, away, across, kappa, beta


def local_solve(levels, rows, read, u_ref, b_ref, rp_ref, a_ref, c_ref):
    for tracer in range(TRACERS):
        carried = None
        for k in range(levels):
            here = read(tracer, k) * span(rp_ref, k, rows)
            if k:
                here = here + span(a_ref, k, rows) * carried
            u_ref[pl.ds((tracer * levels + k) * rows, rows), :] = here
            carried = here
        b_ref[pl.ds((TRACERS + tracer) * rows, rows), :] = carried
        for k in range(levels - 2, -1, -1):
            carried = span(u_ref, tracer * levels + k, rows) + span(c_ref, k, rows) * carried
            u_ref[pl.ds((tracer * levels + k) * rows, rows), :] = carried
        b_ref[pl.ds(tracer * rows, rows), :] = carried


def first_kernel(levels, places, strip, *refs):
    parts, refs = refs[:places], refs[places:]
    adj_ref, u_ref, b_ref, alpha_ref, gamma_ref, static_ref, rp_ref, a_ref, c_ref, t_ref, tv_ref, tw_ref, i_ref, x_ref = refs
    rows = strip * places
    me = lax.axis_index("lev")
    for place in range(places):

        @pl.when(me == place)
        def _():
            for distance in range(places):
                offset = (place ^ distance) * strip
                part = parts[distance]
                for k in range(levels):
                    t_ref[pl.ds(k * rows + offset, strip), :] = part[k]
                dry = {0: 0, places - 1: levels}.get(place)
                for k in range(levels + 1):
                    value = part[levels + k]
                    if k == dry:
                        x_ref[pl.ds(2 * rows + offset, strip), :] = value
                        value = jnp.zeros_like(value)
                    i_ref[pl.ds(k * rows + offset, strip), :] = value
                if dry is None:
                    x_ref[pl.ds(2 * rows + offset, strip), :] = jnp.zeros_like(part[0])
                for n in range(2):
                    x_ref[pl.ds(n * rows + offset, strip), :] = part[2 * levels + 1 + n]

    inner = span(i_ref, 0, rows)
    high = span(t_ref, 0, rows) + inner
    low = jnp.ones_like(high)
    v = None
    for k in range(levels):
        outer = span(i_ref, k + 1, rows)
        ahead = high + outer * low
        rp = low / ahead
        a = inner * rp
        at = pl.ds(k * rows, rows)
        rp_ref[at, :] = rp
        a_ref[at, :] = a
        c_ref[at, :] = outer * rp
        v = a * v if k else a
        tv_ref[at, :] = v
        if k < levels - 1:
            high = span(t_ref, k + 1, rows) * ahead + outer * high
            low = ahead
            inner = outer
    w = span(c_ref, levels - 1, rows)
    v_last, w_last = v, w
    for k in range(levels - 1, -1, -1):
        at = pl.ds(k * rows, rows)
        if k < levels - 1:
            c = span(c_ref, k, rows)
            v = span(tv_ref, k, rows) + c * v
            w = c * w
        t = span(t_ref, k, rows)
        tv_ref[at, :] = t * v
        tw_ref[at, :] = t * w
    is_upper = me < 2
    at_end = (me >> 1) == (me & 1)
    first, second, third = (span(x_ref, n, rows) for n in range(3))
    det, _, across, kappa, beta = pair_factors(first, (v, v_last, w, w_last), is_upper)
    far_det = 1.0 / (1.0 - beta * second)
    bridge = second * far_det
    reach = det * across * bridge
    one, zero = jnp.ones_like(det), jnp.zeros_like(det)
    inner = (
        bridge, bridge * kappa * first, bridge * kappa, far_det, det * first, det, det * first * across,
        one, kappa * first, reach, det + reach * kappa * first,
    )
    ends = (first, zero, one, second, zero, zero, zero, third, zero, one, zero)
    for n, (x, y) in enumerate(zip(ends, inner)):
        static_ref[pl.ds(n * rows, rows), :] = jnp.where(at_end, x, y)
    local_solve(
        levels, rows, lambda tracer, k: span(adj_ref, tracer * levels + k, rows), u_ref, b_ref, rp_ref, a_ref, c_ref
    )
    own_shares(rows, b_ref, static_ref, alpha_ref, gamma_ref)


def near_and_away(rows, b_ref, tracer):
    is_upper = lax.axis_index("lev") < 2
    first, last = span(b_ref, tracer, rows), span(b_ref, TRACERS + tracer, rows)
    return jnp.where(is_upper, last, first), jnp.where(is_upper, first, last)


def own_shares(rows, b_ref, static_ref, alpha_ref, gamma_ref):
    for tracer in range(TRACERS):
        near, away = near_and_away(rows, b_ref, tracer)
        at = pl.ds(tracer * rows, rows)
        alpha_ref[at, :] = span(static_ref, 7, rows) * near + span(static_ref, 8, rows) * away
        gamma_ref[at, :] = span(static_ref, 9, rows) * near + span(static_ref, 10, rows) * away


def edges_kernel(levels, rows, u_ref, t_ref, tv_ref, tw_ref, mask_ref, pack_ref, line_ref, held_ref):
    lane = lax.broadcasted_iota(jnp.int32, (rows, 128), 1)
    for part, source in enumerate((u_ref, tv_ref, tw_ref)):
        packed = jnp.zeros((rows, 128), jnp.float32)
        count = levels * (TRACERS if part == 0 else 1)
        for j in range(count):
            k = j % levels
            value = span(mask_ref, k, rows).astype(jnp.float32) * span(source, j, rows)
            if part == 0:
                value = value * span(t_ref, k, rows)
            held_ref[pl.ds(j * rows, rows), :] = value
            packed = jnp.where((lane >> 1) == j, pltpu.roll(value, 2 * j + 1, 1), packed)
        if part:
            for tracer in range(1, TRACERS):
                packed = jnp.where(
                    (lane >> 1) >= tracer * levels, pltpu.roll(packed, 2 * levels, 1), packed
                )
        pack_ref[pl.ds(part * rows, rows), :] = packed
        for side in range(2):
            for tracer in range(TRACERS):
                first = (tracer if part == 0 else 0) * levels * rows + side * (rows - 1)
                line_ref[pl.ds((part * 2 + side) * 48 + tracer * 24, levels), :] = held_ref[
                    pl.ds(first, levels, stride=rows), :
                ]


def send_kernel(levels, rows, lat_two_ways, fold_apart, *refs):
    mine_ref, other_ref, far_ref, more_ref, static_ref, pack_ref, line_ref, stencil_ref, source_ref = refs[:9]
    out_refs, fold_ref = refs[9:-1], refs[-1]
    outer_ref, lon_ref, lat_ref = out_refs[:3]
    is_upper = lax.axis_index("lev") < 2
    lane = lax.broadcasted_iota(jnp.int32, (rows, 128), 1)
    lat_odd = (lax.axis_index("lat") & 1) == 1
    weight = stencil_ref[pl.ds(3 * levels * rows + rows - 1, levels, stride=rows), :]
    fold_ref[...] = jnp.zeros_like(fold_ref)
    sides = []
    for tracer in range(TRACERS):
        near, away = near_and_away(rows, mine_ref, tracer)
        gamma = span(other_ref, tracer, rows)
        far = span(far_ref, tracer, rows) + span(more_ref, tracer, rows)
        e = [span(static_ref, n, rows) for n in range(7)]
        inward = e[0] * near + e[1] * away + e[2] * gamma + e[3] * far
        outward = e[4] * away + e[5] * gamma + e[6] * inward
        previous = jnp.where(is_upper, outward, inward)
        following = jnp.where(is_upper, inward, outward)
        outer_ref[pl.ds(tracer * rows, rows), :] = previous
        outer_ref[pl.ds((TRACERS + tracer) * rows, rows), :] = following
        ends = []
        for value in (previous, following):
            west = jnp.broadcast_to(value[:, 0:1], (rows, 128))
            east = jnp.broadcast_to(value[:, 127:128], (rows, 128))
            ends.append(jnp.where((lane & 1) == 0, east, west))
        sides.append(ends)
        lines = []
        for side, row in ((0, 0), (1, rows - 1)):
            at = [pl.ds((part * 2 + side) * 48 + tracer * 24, levels) for part in range(3)]
            lines.append(
                line_ref[at[0], :]
                + line_ref[at[1], :] * previous[row : row + 1, :]
                + line_ref[at[2], :] * following[row : row + 1, :]
            )
        first, last = lines
        at = pl.ds(tracer * 24, levels)
        lat_ref[at, :] = jnp.where(lat_odd, first, last)
        if lat_two_ways:
            out_refs[3][at, :] = jnp.where(lat_odd, last, first)
        fold_ref[at, :] = weight * last
    previous, following = sides[0]
    for tracer in range(1, TRACERS):
        later = (lane >> 1) >= tracer * levels
        previous = jnp.where(later, sides[tracer][0], previous)
        following = jnp.where(later, sides[tracer][1], following)
    lon_ref[pl.ds(0, rows), :] = (
        span(pack_ref, 0, rows) + span(pack_ref, 1, rows) * previous + span(pack_ref, 2, rows) * following
    )
    source = source_ref[...]
    for i in range(TRACERS * 3):
        moved = jnp.take_along_axis(fold_ref[pl.ds(i * 8, 8), :], source, axis=1)
        if fold_apart:
            out_refs[-1][pl.ds(i * 8, 8), :] = moved
        else:
            lon_ref[pl.ds(rows + i * 8, 8), :] = moved


def inside_kernel(levels, rows, u_ref, t_ref, tv_ref, tw_ref, outer_ref, mask_ref, stencil_ref, out_ref, side_ref, masked_ref):
    stride = rows + 8
    lane = lax.broadcasted_iota(jnp.int32, (rows, 128), 1)
    nothing = jnp.zeros((levels, 128), jnp.float32)
    for k in range(levels):
        mask = span(mask_ref, k, rows).astype(jnp.float32)
        west, east = span(stencil_ref, 2 * levels + k, rows), span(stencil_ref, levels + k, rows)
        side_ref[pl.ds(k * rows, rows), :] = mask * jnp.where(lane == 0, west, jnp.where(lane == 127, east, 0.0))
    for tracer in range(TRACERS):
        masked_ref[pl.ds(tracer * levels * stride + 7, levels, stride=stride), :] = nothing
        masked_ref[pl.ds((tracer * levels + 1) * stride, levels, stride=stride), :] = nothing
        previous, following = span(outer_ref, tracer, rows), span(outer_ref, TRACERS + tracer, rows)
        for k in range(levels):
            j = tracer * levels + k
            vertical = (
                span(t_ref, k, rows) * span(u_ref, j, rows)
                + span(tv_ref, k, rows) * previous
                + span(tw_ref, k, rows) * following
            )
            mask = span(mask_ref, k, rows).astype(jnp.float32)
            masked = mask * vertical
            masked_ref[pl.ds(j * stride + 8, rows), :] = masked
            from_north = masked_ref[pl.ds(j * stride + 9, rows), :]
            from_south = masked_ref[pl.ds(j * stride + 7, rows), :]
            from_east = jnp.where(lane == 127, 0.0, pltpu.roll(masked, 127, 1))
            from_west = jnp.where(lane == 0, 0.0, pltpu.roll(masked, 1, 1))
            weight = [span(stencil_ref, i * levels + k, rows) for i in range(5)]
            tendency = (
                weight[0] * masked
                + weight[1] * from_east
                + weight[2] * from_west
                + weight[3] * from_north
                + weight[4] * from_south
            )
            out_ref[pl.ds(j * rows, rows), :] = vertical + mask * tendency


def outside_parts(levels, rows, lat_two_ways, fold_apart, refs, line_ref):
    inside_ref, side_ref, mask_ref, stencil_ref, wide_ref, near_ref, lat_ref = refs[:7]
    lon_odd = (lax.axis_index("lon") & 1) == 1
    lat_odd = (lax.axis_index("lat") & 1) == 1
    is_top = lax.axis_index("lat") == lax.axis_size("lat") - 1
    lane = lax.broadcasted_iota(jnp.int32, (rows, 128), 1)
    row = lax.broadcasted_iota(jnp.int32, (rows, 128), 0)
    wide, near = wide_ref[pl.ds(0, rows), :], near_ref[...]
    east, west = jnp.where(lon_odd, wide, near), jnp.where(lon_odd, near, wide)
    edges = jnp.where((lane & 1) == 0, pltpu.roll(east, 127, 1), pltpu.roll(west, 1, 1))
    fold_ref, fold_at = (refs[-1], 0) if fold_apart else (wide_ref, rows)

    def line(ref, plane, at):
        return ref[pl.ds(plane * levels * rows + at, levels, stride=rows), :]

    first_mask = line(mask_ref, 0, 0).astype(jnp.float32)
    last_mask = line(mask_ref, 0, rows - 1).astype(jnp.float32)
    to_north, to_south = line(stencil_ref, 3, rows - 1), line(stencil_ref, 4, 0)
    for tracer in range(TRACERS):
        at = pl.ds(tracer * 24, levels)
        halo = lat_ref[at, :]
        back = refs[7][at, :] if lat_two_ways else jnp.zeros_like(halo)
        north, south = jnp.where(lat_odd, back, halo), jnp.where(lat_odd, halo, back)
        folded = jnp.where(is_top, fold_ref[pl.ds(fold_at + tracer * 24, levels), :], 0.0)
        line_ref[at, :] = first_mask * (to_south * south)
        line_ref[pl.ds(48 + tracer * 24, levels), :] = last_mask * (to_north * north + folded)

    def next_adjoint(tracer, k):
        j = tracer * levels + k
        first = line_ref[pl.ds(tracer * 24 + k, 1), :]
        last = line_ref[pl.ds(48 + tracer * 24 + k, 1), :]
        rim = jnp.where(row == 0, first, jnp.where(row == rows - 1, last, 0.0))
        sides = span(side_ref, k, rows) * pltpu.roll(edges, 127 - 2 * j, 1)
        return span(inside_ref, j, rows) + sides + rim

    return next_adjoint


def turn_kernel(levels, rows, lat_two_ways, fold_apart, *refs):
    *refs, rp_ref, a_ref, c_ref, static_ref, u_ref, b_ref, alpha_ref, gamma_ref, line_ref = refs
    read = outside_parts(levels, rows, lat_two_ways, fold_apart, refs, line_ref)
    local_solve(levels, rows, read, u_ref, b_ref, rp_ref, a_ref, c_ref)
    own_shares(rows, b_ref, static_ref, alpha_ref, gamma_ref)


def last_kernel(levels, rows, lat_two_ways, fold_apart, *refs):
    *refs, out_ref, line_ref, held_ref, sems = refs
    read = outside_parts(levels, rows, lat_two_ways, fold_apart, refs, line_ref)
    copies = []
    half = (levels + 1) // 2
    for tracer in range(TRACERS):
        for first, last in ((0, half), (half, levels)):
            for k in range(first, last):
                held_ref[pl.ds((tracer * levels + k) * rows, rows), :] = read(tracer, k)
            at = pl.ds((tracer * levels + first) * rows, (last - first) * rows)
            copy = pltpu.make_async_copy(held_ref.at[at], out_ref.at[at], sems.at[len(copies)])
            copy.start()
            copies.append(copy)
    for copy in copies:
        copy.wait()


def shards(adj_final, stencil, landmask, thickness, diffusivity, level_counts, fold_partner):
    lat_count, lon_count, places = (lax.axis_size(axis) for axis in ("lat", "lon", "lev"))
    _, levels, rows, width = adj_final.shape
    strip = thickness.shape[1]
    assert places == 4 and width == 128 and strip * places == rows and lon_count % 2 == 0 and lat_count % 2 == 0
    assert 2 * TRACERS * levels <= width and levels <= 24
    flat = (TRACERS * levels * rows, width)
    column = (levels * rows, width)
    adj = adj_final.reshape(flat)
    weights = stencil.reshape(5 * levels * rows, width)
    mask = landmask.reshape(column)

    def lev_swap(value, distance):
        return lax.ppermute(value, "lev", [(i, i ^ distance) for i in range(places)])

    near_pairs = [(i, i ^ 1) for i in range(lon_count)]
    wide_pairs = [(i, (i + 1 if i % 2 else i - 1) % lon_count) for i in range(lon_count)]
    fold_pairs = [(i, lon_count - 1 - i) for i in range(lon_count)]
    fold_apart = wide_pairs != fold_pairs
    lat_two_ways = lat_count > 2
    lat_near = [(i, i ^ 1) for i in range(lat_count)]
    lat_wide = [pair for i in range(1, lat_count - 1, 2) for pair in ((i, i + 1), (i + 1, i))]

    own, *parts, near_adj = call(
        functools.partial(pack_kernel, levels, places),
        [(2 * levels + 3, strip, width)] * places + [flat],
        (thickness, diffusivity, level_counts, adj),
        [thickness.shape, (level_counts.shape, jnp.int32)],
        3 + places,
        read_in_place=True,
    )
    parts = [lev_swap(parts[distance - 1], distance) for distance in range(places - 1, 0, -1)][::-1]
    parts = [own] + parts

    targets = fold_partner - (lon_count - 1 - lax.axis_index("lon")) * width
    here = lax.broadcasted_iota(jnp.int32, (width, width), 0)
    hit = targets[:, None] == lax.broadcasted_iota(jnp.int32, (width, width), 1)
    source = jnp.broadcast_to(jnp.sum(jnp.where(hit, here, 0), axis=0)[None], (8, width))

    solved, ends, alpha, gamma, static, rp, a, c, t, tv, tw = call(
        functools.partial(first_kernel, levels, places, strip),
        [flat, (4 * rows, width), (2 * rows, width), (2 * rows, width), (11 * rows, width)] + [column] * 6,
        (*parts, near_adj),
        [((levels + 1) * rows, width), (3 * rows, width)],
    )
    for turn_index in range(STEPS):
        more, far = lev_swap(alpha, 3), lev_swap(alpha, 2)
        other = lev_swap(gamma, 1)
        packs, lines = call(
            functools.partial(edges_kernel, levels, rows),
            [(3 * rows, width), (6 * 48, width)],
            (solved, t, tv, tw, mask),
            [flat],
        )
        messages = [((rows + (0 if fold_apart else 48)), width), (48, width)]
        messages += [(48, width)] * (lat_two_ways + fold_apart)
        outer, lon_message, lat_message, *rest = call(
            functools.partial(send_kernel, levels, rows, lat_two_ways, fold_apart),
            [(2 * TRACERS * rows, width)] + messages,
            (ends, other, far, more, static, packs, lines, weights, source),
            [(48, width)],
        )
        from_lat = lax.ppermute(lat_message, "lat", lat_near)
        from_wide = lax.ppermute(lon_message, "lon", wide_pairs)
        from_near = lax.ppermute(lon_message[:rows], "lon", near_pairs)
        extra = []
        if lat_two_ways:
            extra.append(lax.ppermute(rest[0], "lat", lat_wide))
        if fold_apart:
            extra.append(lax.ppermute(rest[-1], "lon", fold_pairs))
        inside, sides = call(
            functools.partial(inside_kernel, levels, rows),
            [flat, column],
            (solved, t, tv, tw, outer, mask, weights),
            [(TRACERS * levels * (rows + 8) + 8, width)],
        )
        operands = (inside, sides, mask, weights, from_wide, from_near, from_lat, *extra)
        lines_held = (96, width)
        if turn_index < STEPS - 1:
            solved, ends, alpha, gamma = call(
                functools.partial(turn_kernel, levels, rows, lat_two_ways, fold_apart),
                [flat, (4 * rows, width), (2 * rows, width), (2 * rows, width)],
                (*operands, rp, a, c, static),
                [lines_held],
            )
        else:
            out = call(
                functools.partial(last_kernel, levels, rows, lat_two_ways, fold_apart),
                [flat],
                operands,
                [lines_held, flat],
                4,
                write_in_place=True,
            )[0]
    return out.reshape(adj_final.shape)


def solution(mesh):
    in_specs = (
        P(None, "lev", "lat", "lon"),
        P(None, "lev", "lat", "lon"),
        P("lev", "lat", "lon"),
        P(None, ("lat", "lev"), "lon"),
        P(None, ("lat", "lev"), "lon"),
        P(("lat", "lev"), "lon"),
        P("lon"),
    )
    out_specs = P(None, "lev", "lat", "lon")
    return jax.shard_map(shards, mesh=mesh, in_specs=in_specs, out_specs=out_specs, check_vma=False)
```

profile of v0, /device:TPU:0, one launch (start us, length us, event | category | flops | bytes accessed | tf_op | source)
XLA Modules:
  0.0 37.5 jit_solution(15566998076916317905)
XLA Ops:
  0.0 1.2 %shard_map.73 = (f32[39,4,128]{2,1,0:T(4,128)S(1)}, f32[39,4,128]{2,1,0:T(4,128)S(1)}, f32[39,4,128]{2,1,0:T(4,128)S(1)}, f32[39,4,128]{2,1,0:T(4,128)S(1)}, f32[576,128]{1,0:T(8,128)S(1)}) custom-call(f32[72,4,128]{2,1,0:T(4,128)} %thickness_ref.1, f32[72,4,128]{2,1,0:T(4,128)} %diffusivity_ref.1, s32[4,128]{1,0:T(4,128)} %counts_ref.1, f32[576,128]{1,0:T(8,128)} %bitcast.16), custom_call_target="tpu_custom_call" | custom-call | tf_op jit(solution)/shard_map/pallas_call | solution.py:18
  1.2 3.1 %collective-permute-start = (f32[39,4,128]{2,1,0:T(4,128)S(1)}, f32[39,4,128]{2,1,0:T(4,128)S(1)}, u32[]{:S(2)}, u32[]{:S(2)}) collective-permute-start(f32[39,4,128]{2,1,0:T(4,128)S(1)} %get-tuple-element.40), channel_id=1, source_target_pairs={{0,1},{1,0},{2,3},{3,2},{4,5},{5,4},{6,7},{7,6},{8,9},{9,8},{10,11... | collective-permute-start | bytes 239624 | tf_op jit(solution)/shard_map/ppermute | solution.py:414
  4.4 2.6 %collective-permute-start.1 = (f32[39,4,128]{2,1,0:T(4,128)S(1)}, f32[39,4,128]{2,1,0:T(4,128)S(1)}, u32[]{:S(2)}, u32[]{:S(2)}) collective-permute-start(f32[39,4,128]{2,1,0:T(4,128)S(1)} %get-tuple-element.41), channel_id=1, source_target_pairs={{0,2},{1,3},{2,0},{3,1},{4,6},{5,7},{6,4},{7,5},{8,10},{9,11},{10,... | collective-permute-start | bytes 239624 | tf_op jit(solution)/shard_map/ppermute | solution.py:414
  7.0 0.0 collective-permute-start.2
  7.0 0.0 copy-start.2
  7.0 0.0 copy-start.1
  7.0 0.7 %copy-done.2 = s32[128]{0:T(128)S(1)} copy-done((s32[128]{0:T(128)S(1)}, s32[128]{0:T(128)}, u32[]{:S(2)}) %copy-start.2) | copy-done | bytes 536
  7.6 0.0 collective-permute-done.refs_1_
  7.6 5.8 %collective-permute-done.1.refs_2_ = f32[39,4,128]{2,1,0:T(4,128)S(1)} collective-permute-done((f32[39,4,128]{2,1,0:T(4,128)S(1)}, f32[39,4,128]{2,1,0:T(4,128)S(1)}, u32[]{:S(2)}, u32[]{:S(2)}) %collective-permute-start.1) | collective-permute-done | bytes 79904 | tf_op jit(solution)/shard_map/ppermute | solution.py:414
  13.4 0.0 collective-permute-done.2.refs_3_
  13.4 0.0 copy-start
  13.4 0.3 shard_map.74
  13.7 2.5 %collective-permute-start.4 = (f32[32,128]{1,0:T(8,128)S(1)}, f32[32,128]{1,0:T(8,128)S(1)}, u32[]{:S(2)}, u32[]{:S(2)}) collective-permute-start(f32[32,128]{1,0:T(8,128)S(1)} %get-tuple-element.50), channel_id=1, source_target_pairs={{0,2},{1,3},{2,0},{3,1},{4,6},{5,7},{6,4},{7,5},{8,10},{9,11},{10,... | collective-permute-start | bytes 49160 | tf_op jit(solution)/shard_map/ppermute | solution.py:414
  16.2 1.4 %collective-permute-start.5 = (f32[32,128]{1,0:T(8,128)S(1)}, f32[32,128]{1,0:T(8,128)S(1)}, u32[]{:S(2)}, u32[]{:S(2)}) collective-permute-start(f32[32,128]{1,0:T(8,128)S(1)} %get-tuple-element.50), channel_id=1, source_target_pairs={{0,3},{1,2},{2,1},{3,0},{4,7},{5,6},{6,5},{7,4},{8,11},{9,10},{10,... | collective-permute-start | bytes 49160 | tf_op jit(solution)/shard_map/ppermute | solution.py:414
  17.5 0.0 collective-permute-start.3
  17.5 0.1 select_reduce_fusion
  17.6 0.0 copy-done.1
  17.6 0.3 shard_map.75
  18.0 0.4 %collective-permute-done.4.refs_2_ = f32[32,128]{1,0:T(8,128)S(1)} collective-permute-done((f32[32,128]{1,0:T(8,128)S(1)}, f32[32,128]{1,0:T(8,128)S(1)}, u32[]{:S(2)}, u32[]{:S(2)}) %collective-permute-start.4) | collective-permute-done | bytes 16416 | tf_op jit(solution)/shard_map/ppermute | solution.py:414
  18.4 3.3 %collective-permute-done.5.refs_3_ = f32[32,128]{1,0:T(8,128)S(1)} collective-permute-done((f32[32,128]{1,0:T(8,128)S(1)}, f32[32,128]{1,0:T(8,128)S(1)}, u32[]{:S(2)}, u32[]{:S(2)}) %collective-permute-start.5) | collective-permute-done | bytes 16416 | tf_op jit(solution)/shard_map/ppermute | solution.py:414
  21.7 0.0 collective-permute-done.3.refs_1_
  21.7 0.0 copy-done
  21.7 0.1 shard_map.76
  21.9 0.1 collective-permute-start.6
  21.9 1.6 %collective-permute-start.8 = (f32[48,128]{1,0:T(8,128)S(1)}, f32[48,128]{1,0:T(8,128)S(1)}, u32[]{:S(2)}, u32[]{:S(2)}) collective-permute-start(f32[48,128]{1,0:T(8,128)S(1)} %get-tuple-element.58), channel_id=1, source_target_pairs={{0,16},{16,0},{1,17},{17,1},{2,18},{18,2},{3,19},{19,3},{4,20},{20... | collective-permute-start | bytes 73736 | tf_op jit(solution)/shard_map/ppermute | solution.py:463
  23.5 1.3 %collective-permute-start.7 = (f32[16,128]{1,0:T(8,128)S(1)}, f32[16,128]{1,0:T(8,128)S(1)}, u32[]{:S(2)}, u32[]{:S(2)}) collective-permute-start(f32[16,128]{1,0:T(8,128)S(1)} %slice.6), channel_id=1, source_target_pairs={{0,4},{4,0},{8,12},{12,8},{1,5},{5,1},{9,13},{13,9},{2,6},{6,2},{1... | collective-permute-start | bytes 24584 | tf_op jit(solution)/shard_map/ppermute | solution.py:465
  24.8 0.4 %shard_map.77 = (f32[576,128]{1,0:T(8,128)S(1)}, f32[288,128]{1,0:T(8,128)S(1)}) custom-call(f32[576,128]{1,0:T(8,128)S(1)} %get-tuple-element.44.u_ref, f32[288,128]{1,0:T(8,128)S(1)} %get-tuple-element.45.t_ref, f32[288,128]{1,0:T(8,128)S(1)} %get-tuple-element.46.tv_ref, f32[288,128]{1,0:T(8,128)S(1)} %get-tuple-element.47.tw_ref, ...), custom_call_target="tpu_custom_call" | custom-call | tf_op jit(solution)/shard_map/pallas_call | solution.py:18
  25.2 0.4 %collective-permute-done.7.refs_5_ = f32[16,128]{1,0:T(8,128)S(1)} collective-permute-done((f32[16,128]{1,0:T(8,128)S(1)}, f32[16,128]{1,0:T(8,128)S(1)}, u32[]{:S(2)}, u32[]{:S(2)}) %collective-permute-start.7) | collective-permute-done | bytes 8224 | tf_op jit(solution)/shard_map/ppermute | solution.py:465
  25.6 0.2 collective-permute-done.8.refs_6_
  25.8 0.0 collective-permute-done.6.refs_4_
  25.8 0.3 shard_map.78
  26.1 0.8 %collective-permute-start.10 = (f32[32,128]{1,0:T(8,128)S(1)}, f32[32,128]{1,0:T(8,128)S(1)}, u32[]{:S(2)}, u32[]{:S(2)}) collective-permute-start(f32[32,128]{1,0:T(8,128)S(1)} %get-tuple-element.65), channel_id=1, source_target_pairs={{0,2},{1,3},{2,0},{3,1},{4,6},{5,7},{6,4},{7,5},{8,10},{9,11},{10,... | collective-permute-start | bytes 49160 | tf_op jit(solution)/shard_map/ppermute | solution.py:414
  26.9 1.4 %collective-permute-start.11 = (f32[32,128]{1,0:T(8,128)S(1)}, f32[32,128]{1,0:T(8,128)S(1)}, u32[]{:S(2)}, u32[]{:S(2)}) collective-permute-start(f32[32,128]{1,0:T(8,128)S(1)} %get-tuple-element.65), channel_id=1, source_target_pairs={{0,3},{1,2},{2,1},{3,0},{4,7},{5,6},{6,5},{7,4},{8,11},{9,10},{10,... | collective-permute-start | bytes 49160 | tf_op jit(solution)/shard_map/ppermute | solution.py:414
  28.3 1.4 %collective-permute-start.9 = (f32[32,128]{1,0:T(8,128)S(1)}, f32[32,128]{1,0:T(8,128)S(1)}, u32[]{:S(2)}, u32[]{:S(2)}) collective-permute-start(f32[32,128]{1,0:T(8,128)S(1)} %get-tuple-element.64), channel_id=1, source_target_pairs={{0,1},{1,0},{2,3},{3,2},{4,5},{5,4},{6,7},{7,6},{8,9},{9,8},{10,11... | collective-permute-start | bytes 49160 | tf_op jit(solution)/shard_map/ppermute | solution.py:414
  29.7 0.3 shard_map.79
  30.0 0.8 %collective-permute-done.10.refs_2_ = f32[32,128]{1,0:T(8,128)S(1)} collective-permute-done((f32[32,128]{1,0:T(8,128)S(1)}, f32[32,128]{1,0:T(8,128)S(1)}, u32[]{:S(2)}, u32[]{:S(2)}) %collective-permute-start.10) | collective-permute-done | bytes 16416 | tf_op jit(solution)/shard_map/ppermute | solution.py:414
  30.8 1.6 %collective-permute-done.11.refs_3_ = f32[32,128]{1,0:T(8,128)S(1)} collective-permute-done((f32[32,128]{1,0:T(8,128)S(1)}, f32[32,128]{1,0:T(8,128)S(1)}, u32[]{:S(2)}, u32[]{:S(2)}) %collective-permute-start.11) | collective-permute-done | bytes 16416 | tf_op jit(solution)/shard_map/ppermute | solution.py:414
  32.5 0.0 collective-permute-done.9.refs_1_
  32.5 0.1 shard_map.80
  32.6 0.1 collective-permute-start.12
  32.7 1.6 %collective-permute-start.14 = (f32[48,128]{1,0:T(8,128)S(1)}, f32[48,128]{1,0:T(8,128)S(1)}, u32[]{:S(2)}, u32[]{:S(2)}) collective-permute-start(f32[48,128]{1,0:T(8,128)S(1)} %get-tuple-element.72), channel_id=1, source_target_pairs={{0,16},{16,0},{1,17},{17,1},{2,18},{18,2},{3,19},{19,3},{4,20},{20... | collective-permute-start | bytes 73736 | tf_op jit(solution)/shard_map/ppermute | solution.py:463
  34.2 1.3 %collective-permute-start.13 = (f32[16,128]{1,0:T(8,128)S(1)}, f32[16,128]{1,0:T(8,128)S(1)}, u32[]{:S(2)}, u32[]{:S(2)}) collective-permute-start(f32[16,128]{1,0:T(8,128)S(1)} %slice.7), channel_id=1, source_target_pairs={{0,4},{4,0},{8,12},{12,8},{1,5},{5,1},{9,13},{13,9},{2,6},{6,2},{1... | collective-permute-start | bytes 24584 | tf_op jit(solution)/shard_map/ppermute | solution.py:465
  35.5 0.4 %shard_map.81 = (f32[576,128]{1,0:T(8,128)S(1)}, f32[288,128]{1,0:T(8,128)S(1)}) custom-call(f32[576,128]{1,0:T(8,128)S(1)} %get-tuple-element.62.u_ref, f32[288,128]{1,0:T(8,128)S(1)} %get-tuple-element.45.t_ref, f32[288,128]{1,0:T(8,128)S(1)} %get-tuple-element.46.tv_ref, f32[288,128]{1,0:T(8,128)S(1)} %get-tuple-element.47.tw_ref, ...), custom_call_target="tpu_custom_call" | custom-call | tf_op jit(solution)/shard_map/pallas_call | solution.py:18
  35.9 0.4 %collective-permute-done.13.refs_5_ = f32[16,128]{1,0:T(8,128)S(1)} collective-permute-done((f32[16,128]{1,0:T(8,128)S(1)}, f32[16,128]{1,0:T(8,128)S(1)}, u32[]{:S(2)}, u32[]{:S(2)}) %collective-permute-start.13) | collective-permute-done | bytes 8224 | tf_op jit(solution)/shard_map/ppermute | solution.py:465
  36.3 0.2 collective-permute-done.14.refs_6_
  36.6 0.0 collective-permute-done.12.refs_4_
  36.6 0.9 %shard_map.82 = f32[576,128]{1,0:T(8,128)} custom-call(f32[576,128]{1,0:T(8,128)S(1)} %get-tuple-element.69.refs_0_, f32[288,128]{1,0:T(8,128)S(1)} %get-tuple-element.70.refs_1_, s32[288,128]{1,0:T(8,128)S(1)} %bitcast.15, f32[1440,128]{1,0:T(8,128)S(1)} %bitcast.9, f32[64,128]{1,0:T(8,128)S(1)} %collective-permute-done.12.refs_4_, ...), custom_call_target="tpu_custom_call" | custom-call | tf_op jit(solution)/shard_map/pallas_call | solution.py:18
  (4 shorter events, 0.0 us)
Async XLA Ops:
  1.2 6.4 %collective-permute-start = (f32[39,4,128]{2,1,0:T(4,128)S(1)}, f32[39,4,128]{2,1,0:T(4,128)S(1)}, u32[]{:S(2)}, u32[]{:S(2)}) collective-permute-start(f32[39,4,128]{2,1,0:T(4,128)S(1)} %get-tuple-element.40), channel_id=1, source_target_pairs={{0,1},{1,0},{2,3},{3,2},{4,5},{5,4},{6,7},{7,6},{8,9},{9,8},{10,11... | collective-permute-start | bytes 239624 | tf_op jit(solution)/shard_map/ppermute | solution.py:414
  4.4 9.0 %collective-permute-start.1 = (f32[39,4,128]{2,1,0:T(4,128)S(1)}, f32[39,4,128]{2,1,0:T(4,128)S(1)}, u32[]{:S(2)}, u32[]{:S(2)}) collective-permute-start(f32[39,4,128]{2,1,0:T(4,128)S(1)} %get-tuple-element.41), channel_id=1, source_target_pairs={{0,2},{1,3},{2,0},{3,1},{4,6},{5,7},{6,4},{7,5},{8,10},{9,11},{10,... | collective-permute-start | bytes 239624 | tf_op jit(solution)/shard_map/ppermute | solution.py:414
  7.0 6.5 %collective-permute-start.2 = (f32[39,4,128]{2,1,0:T(4,128)S(1)}, f32[39,4,128]{2,1,0:T(4,128)S(1)}, u32[]{:S(2)}, u32[]{:S(2)}) collective-permute-start(f32[39,4,128]{2,1,0:T(4,128)S(1)} %get-tuple-element.42), channel_id=1, source_target_pairs={{0,3},{1,2},{2,1},{3,0},{4,7},{5,6},{6,5},{7,4},{8,11},{9,10},{10,... | collective-permute-start | bytes 239624 | tf_op jit(solution)/shard_map/ppermute | solution.py:414
  7.0 0.7 %copy-start.2 = (s32[128]{0:T(128)S(1)}, s32[128]{0:T(128)}, u32[]{:S(2)}) copy-start(s32[128]{0:T(128)} %param.13) | copy-start | bytes 1540
  7.0 10.7 %copy-start.1 = (s32[18,16,128]{2,1,0:T(8,128)S(1)}, s32[18,16,128]{2,1,0:T(8,128)}, u32[]{:S(2)}) copy-start(s32[18,16,128]{2,1,0:T(8,128)} %param.9) | copy-start | bytes 442372
  13.4 8.3 %copy-start = (f32[5,18,16,128]{3,2,1,0:T(8,128)S(1)}, f32[5,18,16,128]{3,2,1,0:T(8,128)}, u32[]{:S(2)}) copy-start(f32[5,18,16,128]{3,2,1,0:T(8,128)} %param.8) | copy-start | bytes 2211844
  13.7 4.7 %collective-permute-start.4 = (f32[32,128]{1,0:T(8,128)S(1)}, f32[32,128]{1,0:T(8,128)S(1)}, u32[]{:S(2)}, u32[]{:S(2)}) collective-permute-start(f32[32,128]{1,0:T(8,128)S(1)} %get-tuple-element.50), channel_id=1, source_target_pairs={{0,2},{1,3},{2,0},{3,1},{4,6},{5,7},{6,4},{7,5},{8,10},{9,11},{10,... | collective-permute-start | bytes 49160 | tf_op jit(solution)/shard_map/ppermute | solution.py:414
  16.2 5.5 %collective-permute-start.5 = (f32[32,128]{1,0:T(8,128)S(1)}, f32[32,128]{1,0:T(8,128)S(1)}, u32[]{:S(2)}, u32[]{:S(2)}) collective-permute-start(f32[32,128]{1,0:T(8,128)S(1)} %get-tuple-element.50), channel_id=1, source_target_pairs={{0,3},{1,2},{2,1},{3,0},{4,7},{5,6},{6,5},{7,4},{8,11},{9,10},{10,... | collective-permute-start | bytes 49160 | tf_op jit(solution)/shard_map/ppermute | solution.py:414
  17.5 4.2 %collective-permute-start.3 = (f32[32,128]{1,0:T(8,128)S(1)}, f32[32,128]{1,0:T(8,128)S(1)}, u32[]{:S(2)}, u32[]{:S(2)}) collective-permute-start(f32[32,128]{1,0:T(8,128)S(1)} %get-tuple-element.49), channel_id=1, source_target_pairs={{0,1},{1,0},{2,3},{3,2},{4,5},{5,4},{6,7},{7,6},{8,9},{9,8},{10,11... | collective-permute-start | bytes 49160 | tf_op jit(solution)/shard_map/ppermute | solution.py:414
  21.9 4.0 %collective-permute-start.6 = (f32[64,128]{1,0:T(8,128)S(1)}, f32[64,128]{1,0:T(8,128)S(1)}, u32[]{:S(2)}, u32[]{:S(2)}) collective-permute-start(f32[64,128]{1,0:T(8,128)S(1)} %get-tuple-element.57), channel_id=1, source_target_pairs={{0,12},{4,8},{8,4},{12,0},{1,13},{5,9},{9,5},{13,1},{2,14},{6,10},... | collective-permute-start | bytes 98312 | tf_op jit(solution)/shard_map/ppermute | solution.py:464
  21.9 3.9 %collective-permute-start.8 = (f32[48,128]{1,0:T(8,128)S(1)}, f32[48,128]{1,0:T(8,128)S(1)}, u32[]{:S(2)}, u32[]{:S(2)}) collective-permute-start(f32[48,128]{1,0:T(8,128)S(1)} %get-tuple-element.58), channel_id=1, source_target_pairs={{0,16},{16,0},{1,17},{17,1},{2,18},{18,2},{3,19},{19,3},{4,20},{20... | collective-permute-start | bytes 73736 | tf_op jit(solution)/shard_map/ppermute | solution.py:463
  23.5 2.1 %collective-permute-start.7 = (f32[16,128]{1,0:T(8,128)S(1)}, f32[16,128]{1,0:T(8,128)S(1)}, u32[]{:S(2)}, u32[]{:S(2)}) collective-permute-start(f32[16,128]{1,0:T(8,128)S(1)} %slice.6), channel_id=1, source_target_pairs={{0,4},{4,0},{8,12},{12,8},{1,5},{5,1},{9,13},{13,9},{2,6},{6,2},{1... | collective-permute-start | bytes 24584 | tf_op jit(solution)/shard_map/ppermute | solution.py:465
  26.1 4.7 %collective-permute-start.10 = (f32[32,128]{1,0:T(8,128)S(1)}, f32[32,128]{1,0:T(8,128)S(1)}, u32[]{:S(2)}, u32[]{:S(2)}) collective-permute-start(f32[32,128]{1,0:T(8,128)S(1)} %get-tuple-element.65), channel_id=1, source_target_pairs={{0,2},{1,3},{2,0},{3,1},{4,6},{5,7},{6,4},{7,5},{8,10},{9,11},{10,... | collective-permute-start | bytes 49160 | tf_op jit(solution)/shard_map/ppermute | solution.py:414
  26.9 5.5 %collective-permute-start.11 = (f32[32,128]{1,0:T(8,128)S(1)}, f32[32,128]{1,0:T(8,128)S(1)}, u32[]{:S(2)}, u32[]{:S(2)}) collective-permute-start(f32[32,128]{1,0:T(8,128)S(1)} %get-tuple-element.65), channel_id=1, source_target_pairs={{0,3},{1,2},{2,1},{3,0},{4,7},{5,6},{6,5},{7,4},{8,11},{9,10},{10,... | collective-permute-start | bytes 49160 | tf_op jit(solution)/shard_map/ppermute | solution.py:414
  28.3 4.2 %collective-permute-start.9 = (f32[32,128]{1,0:T(8,128)S(1)}, f32[32,128]{1,0:T(8,128)S(1)}, u32[]{:S(2)}, u32[]{:S(2)}) collective-permute-start(f32[32,128]{1,0:T(8,128)S(1)} %get-tuple-element.64), channel_id=1, source_target_pairs={{0,1},{1,0},{2,3},{3,2},{4,5},{5,4},{6,7},{7,6},{8,9},{9,8},{10,11... | collective-permute-start | bytes 49160 | tf_op jit(solution)/shard_map/ppermute | solution.py:414
  32.6 4.0 %collective-permute-start.12 = (f32[64,128]{1,0:T(8,128)S(1)}, f32[64,128]{1,0:T(8,128)S(1)}, u32[]{:S(2)}, u32[]{:S(2)}) collective-permute-start(f32[64,128]{1,0:T(8,128)S(1)} %get-tuple-element.71), channel_id=1, source_target_pairs={{0,12},{4,8},{8,4},{12,0},{1,13},{5,9},{9,5},{13,1},{2,14},{6,10},... | collective-permute-start | bytes 98312 | tf_op jit(solution)/shard_map/ppermute | solution.py:464
  32.7 3.9 %collective-permute-start.14 = (f32[48,128]{1,0:T(8,128)S(1)}, f32[48,128]{1,0:T(8,128)S(1)}, u32[]{:S(2)}, u32[]{:S(2)}) collective-permute-start(f32[48,128]{1,0:T(8,128)S(1)} %get-tuple-element.72), channel_id=1, source_target_pairs={{0,16},{16,0},{1,17},{17,1},{2,18},{18,2},{3,19},{19,3},{4,20},{20... | collective-permute-start | bytes 73736 | tf_op jit(solution)/shard_map/ppermute | solution.py:463
  34.2 2.1 %collective-permute-start.13 = (f32[16,128]{1,0:T(8,128)S(1)}, f32[16,128]{1,0:T(8,128)S(1)}, u32[]{:S(2)}, u32[]{:S(2)}) collective-permute-start(f32[16,128]{1,0:T(8,128)S(1)} %slice.7), channel_id=1, source_target_pairs={{0,4},{4,0},{8,12},{12,8},{1,5},{5,1},{9,13},{13,9},{2,6},{6,2},{1... | collective-permute-start | bytes 24584 | tf_op jit(solution)/shard_map/ppermute | solution.py:465
where the time goes:
time: 37.6 us; the launch traced here: 37.5 us
  starting transfers between devices  18.9 us (50%)
  waiting for transfers between devices  13.3 us (35%)
  Pallas kernels  4.41 us (12%)
  local copies, waits for them, and re-layouts  0.67 us (2%)
    ppermute x9, starting transfers between devices, lev_swap(): lax.ppermute(value, 'lev', [(i, i ^ distance) for i in range(places)])  13.1 us
    ppermute x9, waiting for transfers between devices, lev_swap(): lax.ppermute(value, 'lev', [(i, i ^ distance) for i in range(places)])  12 us
    pallas_call x10, Pallas kernels, call(): pl.pallas_call(kernel, out_shape=[jax.ShapeDtypeStruct(shape, jnp.float32...  4.41 us
    ppermute x2, starting transfers between devices, shards(): from_lat = lax.ppermute(lat_message, 'lat', lat_near)  3.11 us
    ppermute x2, starting transfers between devices, shards(): from_near = lax.ppermute(lon_message[:rows], 'lon', near_pairs)  2.55 us
    ppermute x2, waiting for transfers between devices, shards(): from_near = lax.ppermute(lon_message[:rows], 'lon', near_pairs)  0.86 us
  transfers between devices with their start and end apart: 15, of which 9 were waited for; matrix products, arithmetic and copies ran while one was open for 0% of the time, Pallas kernels for 4%

commit v1 on v0

--- a/solution.py
+++ b/solution.py
@@ -14,16 +14,18 @@
 
 
 def call(kernel, out_shapes, operands, scratch=(), copies=0, read_in_place=False, write_in_place=False):
+    if isinstance(read_in_place, bool):
+        read_in_place = (read_in_place,) * len(operands)
     vmem, any_space = pl.BlockSpec(memory_space=pltpu.VMEM), pl.BlockSpec(memory_space=pltpu.HBM)
     return pl.pallas_call(
         kernel,
         out_shape=[jax.ShapeDtypeStruct(shape, jnp.float32) for shape in out_shapes],
-        in_specs=[any_space if read_in_place else vmem] * len(operands),
+        in_specs=[any_space if in_place else vmem for in_place in read_in_place],
         out_specs=[any_space if write_in_place else vmem] * len(out_shapes),
         scratch_shapes=[pltpu.VMEM(*shape) if isinstance(shape[0], tuple) else pltpu.VMEM(shape, jnp.float32) for shape in scratch]
         + [pltpu.SemaphoreType.DMA((copies,))] * (copies > 0),
         compiler_params=pltpu.CompilerParams(vmem_limit_bytes=GRANT),
-    )(*((pltpu.with_memory_space_constraint(x, pltpu.HBM) for x in operands) if read_in_place else operands))
+    )(*(pltpu.with_memory_space_constraint(x, pltpu.HBM) if i else x for x, i in zip(operands, read_in_place)))
 
 
 def span(ref, index, rows):
@@ -47,20 +49,24 @@
     return i[0] * back_low * scale, i[0] * through * scale, through * i[-1] * scale, i[-1] * low * scale
 
 
-def pack_kernel(levels, places, thickness_ref, diffusivity_ref, counts_ref, adj_ref, *refs):
-    out_refs, (near_adj_ref, held_ref, held_counts_ref, sems) = refs[:places], refs[places:]
+def pack_kernel(levels, places, thickness_ref, diffusivity_ref, counts_ref, *refs):
+    out_refs, (held_ref, held_counts_ref, sems) = refs[:places], refs[places:]
     me = lax.axis_index("lev")
-    ahead = [
-        pltpu.make_async_copy(counts_ref, held_counts_ref, sems.at[0]),
-        pltpu.make_async_copy(diffusivity_ref, held_ref, sems.at[1]),
-    ]
+    counts_copy = pltpu.make_async_copy(counts_ref, held_counts_ref, sems.at[0])
+    counts_copy.start()
+    copies = []
     for distance in range(places):
-        source = thickness_ref.at[pl.ds((me ^ distance) * levels, levels)]
-        ahead.append(pltpu.make_async_copy(source, out_refs[distance].at[pl.ds(0, levels)], sems.at[2 + distance]))
-    ahead.append(pltpu.make_async_copy(adj_ref, near_adj_ref, sems.at[2 + places]))
-    for copy in ahead:
-        copy.start()
-    for copy in ahead[:2]:
+        at = pl.ds((me ^ distance) * levels, levels)
+        copies.append(pltpu.make_async_copy(diffusivity_ref.at[at], held_ref.at[at], sems.at[1 + distance]))
+        copies[-1].start()
+    for distance in range(places):
+        at = pl.ds((me ^ distance) * levels, levels)
+        copies.append(
+            pltpu.make_async_copy(thickness_ref.at[at], out_refs[distance].at[pl.ds(0, levels)], sems.at[1 + places + distance])
+        )
+        copies[-1].start()
+    counts_copy.wait()
+    for copy in copies[:places]:
         copy.wait()
     counts = held_counts_ref[...]
     last = held_ref.shape[0] - 1
@@ -70,7 +76,7 @@
             level = jnp.full(counts.shape, start + k, jnp.int32)
             wet = (level >= 1) & (level < counts)
             out_refs[distance][levels + k] = jnp.where(wet, held_ref[jnp.minimum(start + k, last)], 0.0)
-    for copy in ahead[2:-1]:
+    for copy in copies[places:]:
         copy.wait()
     spikes = [end_values(out_refs[distance], levels) for distance in range(places)]
     at_end = (me >> 1) == (me & 1)
@@ -96,7 +102,12 @@
         out[2 * levels + 2] = jnp.where(ends_here, reach, far_beta)
         out[levels] = jnp.where(place == 0, kappa, out[levels])
         out[2 * levels] = jnp.where(place == places - 1, kappa, out[2 * levels])
-    ahead[-1].wait()
+
+
+def fetch_kernel(after_ref, adj_ref, near_adj_ref, sems):
+    copy = pltpu.make_async_copy(adj_ref, near_adj_ref, sems.at[0])
+    copy.start()
+    copy.wait()
 
 
 def pair_factors(outer_near, inner, is_upper):
@@ -421,14 +432,15 @@
     lat_near = [(i, i ^ 1) for i in range(lat_count)]
     lat_wide = [pair for i in range(1, lat_count - 1, 2) for pair in ((i, i + 1), (i + 1, i))]
 
-    own, *parts, near_adj = call(
+    own, *parts = call(
         functools.partial(pack_kernel, levels, places),
-        [(2 * levels + 3, strip, width)] * places + [flat],
-        (thickness, diffusivity, level_counts, adj),
+        [(2 * levels + 3, strip, width)] * places,
+        (thickness, diffusivity, level_counts),
         [thickness.shape, (level_counts.shape, jnp.int32)],
-        3 + places,
+        1 + 2 * places,
         read_in_place=True,
     )
+    near_adj = call(fetch_kernel, [flat], (own, adj), (), 1, read_in_place=(False, True))[0]
     parts = [lev_swap(parts[distance - 1], distance) for distance in range(places - 1, 0, -1)][::-1]
     parts = [own] + parts
 

time: 37.6 us -> 37.6 us (level)
  waiting for transfers between devices: 13.3 us -> 12.3 us
  Pallas kernels: 4.41 us -> 5.3 us
    ppermute x9, waiting for transfers between devices: 12 us -> 11 us  [lev_swap(): lax.ppermute(value, 'lev', [(i, i ^ distance) for i in range(places)])]
    pallas_call x10 -> x11, Pallas kernels: 4.41 us -> 5.3 us  [call(): pl.pallas_call(kernel, out_shape=[jax.ShapeDtypeStruct(shape, jnp.float32...]
  transfers between devices with their start and end apart: 15 -> 15, of which waited for: 9 -> 9; matrix products, arithmetic and copies ran while one was open for 0% -> 0% of each run, Pallas kernels for 4% -> 6%
where the time goes in v1:
time: 37.6 us; the launch traced here: 37.4 us
  starting transfers between devices  18.9 us (50%)
  waiting for transfers between devices  12.3 us (33%)
  Pallas kernels  5.3 us (14%)
  local copies, waits for them, and re-layouts  0.67 us (2%)
    ppermute x9, starting transfers between devices, lev_swap(): lax.ppermute(value, 'lev', [(i, i ^ distance) for i in range(places)])  13.1 us
    ppermute x9, waiting for transfers between devices, lev_swap(): lax.ppermute(value, 'lev', [(i, i ^ distance) for i in range(places)])  11 us
    pallas_call x11, Pallas kernels, call(): pl.pallas_call(kernel, out_shape=[jax.ShapeDtypeStruct(shape, jnp.float32...  5.3 us
    ppermute x2, starting transfers between devices, shards(): from_lat = lax.ppermute(lat_message, 'lat', lat_near)  3.11 us
    ppermute x2, starting transfers between devices, shards(): from_near = lax.ppermute(lon_message[:rows], 'lon', near_pairs)  2.55 us
    ppermute x2, waiting for transfers between devices, shards(): from_near = lax.ppermute(lon_message[:rows], 'lon', near_pairs)  0.9 us
  transfers between devices with their start and end apart: 15, of which 9 were waited for; matrix products, arithmetic and copies ran while one was open for 0% of the time, Pallas kernels for 6%

profile of v1, /device:TPU:0, one launch (start us, length us, event | category | flops | bytes accessed | tf_op | source)
XLA Modules:
  0.0 37.4 jit_solution(15616838316888117038)
XLA Ops:
  0.0 1.2 %shard_map.73 = (f32[39,4,128]{2,1,0:T(4,128)S(1)}, f32[39,4,128]{2,1,0:T(4,128)S(1)}, f32[39,4,128]{2,1,0:T(4,128)S(1)}, f32[39,4,128]{2,1,0:T(4,128)S(1)}) custom-call(f32[72,4,128]{2,1,0:T(4,128)} %thickness_ref.1, f32[72,4,128]{2,1,0:T(4,128)} %diffusivity_ref.1, s32[4,128]{1,0:T(4,128)} %counts_ref.1), custom_call_target="tpu_custom_call" | custom-call | tf_op jit(solution)/shard_map/pallas_call | solution.py:20
  1.2 3.1 %collective-permute-start = (f32[39,4,128]{2,1,0:T(4,128)S(1)}, f32[39,4,128]{2,1,0:T(4,128)S(1)}, u32[]{:S(2)}, u32[]{:S(2)}) collective-permute-start(f32[39,4,128]{2,1,0:T(4,128)S(1)} %get-tuple-element.39), channel_id=1, source_target_pairs={{0,1},{1,0},{2,3},{3,2},{4,5},{5,4},{6,7},{7,6},{8,9},{9,8},{10,11... | collective-permute-start | bytes 239624 | tf_op jit(solution)/shard_map/ppermute | solution.py:425
  4.3 2.6 %collective-permute-start.1 = (f32[39,4,128]{2,1,0:T(4,128)S(1)}, f32[39,4,128]{2,1,0:T(4,128)S(1)}, u32[]{:S(2)}, u32[]{:S(2)}) collective-permute-start(f32[39,4,128]{2,1,0:T(4,128)S(1)} %get-tuple-element.40), channel_id=1, source_target_pairs={{0,2},{1,3},{2,0},{3,1},{4,6},{5,7},{6,4},{7,5},{8,10},{9,11},{10,... | collective-permute-start | bytes 239624 | tf_op jit(solution)/shard_map/ppermute | solution.py:425
  6.9 0.0 collective-permute-start.2
  6.9 0.0 copy-start.2
  6.9 0.7 %copy-done.2 = s32[128]{0:T(128)S(1)} copy-done((s32[128]{0:T(128)S(1)}, s32[128]{0:T(128)}, u32[]{:S(2)}) %copy-start.2) | copy-done | bytes 536
  7.5 0.0 copy-start.1
  7.5 1.0 %shard_map.74.refs_4_ = f32[576,128]{1,0:T(8,128)S(1)} custom-call(f32[39,4,128]{2,1,0:T(4,128)S(1)} %get-tuple-element.38.after_ref.refs_0_, f32[576,128]{1,0:T(8,128)} %bitcast.16), custom_call_target="tpu_custom_call" | custom-call | tf_op jit(solution)/shard_map/pallas_call | solution.py:20
  8.6 0.0 copy-start
  8.6 0.0 collective-permute-done.refs_1_
  8.6 4.7 %collective-permute-done.1.refs_2_ = f32[39,4,128]{2,1,0:T(4,128)S(1)} collective-permute-done((f32[39,4,128]{2,1,0:T(4,128)S(1)}, f32[39,4,128]{2,1,0:T(4,128)S(1)}, u32[]{:S(2)}, u32[]{:S(2)}) %collective-permute-start.1) | collective-permute-done | bytes 79904 | tf_op jit(solution)/shard_map/ppermute | solution.py:425
  13.3 0.0 collective-permute-done.2.refs_3_
  13.3 0.3 shard_map.75
  13.6 2.5 %collective-permute-start.4 = (f32[32,128]{1,0:T(8,128)S(1)}, f32[32,128]{1,0:T(8,128)S(1)}, u32[]{:S(2)}, u32[]{:S(2)}) collective-permute-start(f32[32,128]{1,0:T(8,128)S(1)} %get-tuple-element.48), channel_id=1, source_target_pairs={{0,2},{1,3},{2,0},{3,1},{4,6},{5,7},{6,4},{7,5},{8,10},{9,11},{10,... | collective-permute-start | bytes 49160 | tf_op jit(solution)/shard_map/ppermute | solution.py:425
  16.1 1.4 %collective-permute-start.5 = (f32[32,128]{1,0:T(8,128)S(1)}, f32[32,128]{1,0:T(8,128)S(1)}, u32[]{:S(2)}, u32[]{:S(2)}) collective-permute-start(f32[32,128]{1,0:T(8,128)S(1)} %get-tuple-element.48), channel_id=1, source_target_pairs={{0,3},{1,2},{2,1},{3,0},{4,7},{5,6},{6,5},{7,4},{8,11},{9,10},{10,... | collective-permute-start | bytes 49160 | tf_op jit(solution)/shard_map/ppermute | solution.py:425
  17.5 0.0 collective-permute-start.3
  17.5 0.1 select_reduce_fusion
  17.6 0.0 copy-done.1
  17.6 0.3 shard_map.76
  17.9 0.4 %collective-permute-done.4.refs_2_ = f32[32,128]{1,0:T(8,128)S(1)} collective-permute-done((f32[32,128]{1,0:T(8,128)S(1)}, f32[32,128]{1,0:T(8,128)S(1)}, u32[]{:S(2)}, u32[]{:S(2)}) %collective-permute-start.4) | collective-permute-done | bytes 16416 | tf_op jit(solution)/shard_map/ppermute | solution.py:425
  18.3 3.3 %collective-permute-done.5.refs_3_ = f32[32,128]{1,0:T(8,128)S(1)} collective-permute-done((f32[32,128]{1,0:T(8,128)S(1)}, f32[32,128]{1,0:T(8,128)S(1)}, u32[]{:S(2)}, u32[]{:S(2)}) %collective-permute-start.5) | collective-permute-done | bytes 16416 | tf_op jit(solution)/shard_map/ppermute | solution.py:425
  21.6 0.0 collective-permute-done.3.refs_1_
  21.7 0.0 copy-done
  21.7 0.1 shard_map.77
  21.8 0.1 collective-permute-start.6
  21.9 1.6 %collective-permute-start.8 = (f32[48,128]{1,0:T(8,128)S(1)}, f32[48,128]{1,0:T(8,128)S(1)}, u32[]{:S(2)}, u32[]{:S(2)}) collective-permute-start(f32[48,128]{1,0:T(8,128)S(1)} %get-tuple-element.56), channel_id=1, source_target_pairs={{0,16},{16,0},{1,17},{17,1},{2,18},{18,2},{3,19},{19,3},{4,20},{20... | collective-permute-start | bytes 73736 | tf_op jit(solution)/shard_map/ppermute | solution.py:475
  23.4 1.3 %collective-permute-start.7 = (f32[16,128]{1,0:T(8,128)S(1)}, f32[16,128]{1,0:T(8,128)S(1)}, u32[]{:S(2)}, u32[]{:S(2)}) collective-permute-start(f32[16,128]{1,0:T(8,128)S(1)} %slice.6), channel_id=1, source_target_pairs={{0,4},{4,0},{8,12},{12,8},{1,5},{5,1},{9,13},{13,9},{2,6},{6,2},{1... | collective-permute-start | bytes 24584 | tf_op jit(solution)/shard_map/ppermute | solution.py:477
  24.7 0.4 shard_map.78
  25.1 0.5 %collective-permute-done.7.refs_5_ = f32[16,128]{1,0:T(8,128)S(1)} collective-permute-done((f32[16,128]{1,0:T(8,128)S(1)}, f32[16,128]{1,0:T(8,128)S(1)}, u32[]{:S(2)}, u32[]{:S(2)}) %collective-permute-start.7) | collective-permute-done | bytes 8224 | tf_op jit(solution)/shard_map/ppermute | solution.py:477
  25.5 0.2 collective-permute-done.8.refs_6_
  25.8 0.0 collective-permute-done.6.refs_4_
  25.8 0.3 shard_map.79
  26.0 0.8 %collective-permute-start.10 = (f32[32,128]{1,0:T(8,128)S(1)}, f32[32,128]{1,0:T(8,128)S(1)}, u32[]{:S(2)}, u32[]{:S(2)}) collective-permute-start(f32[32,128]{1,0:T(8,128)S(1)} %get-tuple-element.63), channel_id=1, source_target_pairs={{0,2},{1,3},{2,0},{3,1},{4,6},{5,7},{6,4},{7,5},{8,10},{9,11},{10,... | collective-permute-start | bytes 49160 | tf_op jit(solution)/shard_map/ppermute | solution.py:425
  26.8 1.4 %collective-permute-start.11 = (f32[32,128]{1,0:T(8,128)S(1)}, f32[32,128]{1,0:T(8,128)S(1)}, u32[]{:S(2)}, u32[]{:S(2)}) collective-permute-start(f32[32,128]{1,0:T(8,128)S(1)} %get-tuple-element.63), channel_id=1, source_target_pairs={{0,3},{1,2},{2,1},{3,0},{4,7},{5,6},{6,5},{7,4},{8,11},{9,10},{10,... | collective-permute-start | bytes 49160 | tf_op jit(solution)/shard_map/ppermute | solution.py:425
  28.2 1.4 %collective-permute-start.9 = (f32[32,128]{1,0:T(8,128)S(1)}, f32[32,128]{1,0:T(8,128)S(1)}, u32[]{:S(2)}, u32[]{:S(2)}) collective-permute-start(f32[32,128]{1,0:T(8,128)S(1)} %get-tuple-element.62), channel_id=1, source_target_pairs={{0,1},{1,0},{2,3},{3,2},{4,5},{5,4},{6,7},{7,6},{8,9},{9,8},{10,11... | collective-permute-start | bytes 49160 | tf_op jit(solution)/shard_map/ppermute | solution.py:425
  29.6 0.3 shard_map.80
  29.9 0.8 %collective-permute-done.10.refs_2_ = f32[32,128]{1,0:T(8,128)S(1)} collective-permute-done((f32[32,128]{1,0:T(8,128)S(1)}, f32[32,128]{1,0:T(8,128)S(1)}, u32[]{:S(2)}, u32[]{:S(2)}) %collective-permute-start.10) | collective-permute-done | bytes 16416 | tf_op jit(solution)/shard_map/ppermute | solution.py:425
  30.7 1.6 %collective-permute-done.11.refs_3_ = f32[32,128]{1,0:T(8,128)S(1)} collective-permute-done((f32[32,128]{1,0:T(8,128)S(1)}, f32[32,128]{1,0:T(8,128)S(1)}, u32[]{:S(2)}, u32[]{:S(2)}) %collective-permute-start.11) | collective-permute-done | bytes 16416 | tf_op jit(solution)/shard_map/ppermute | solution.py:425
  32.4 0.0 collective-permute-done.9.refs_1_
  32.4 0.1 shard_map.81
  32.5 0.1 collective-permute-start.12
  32.6 1.6 %collective-permute-start.14 = (f32[48,128]{1,0:T(8,128)S(1)}, f32[48,128]{1,0:T(8,128)S(1)}, u32[]{:S(2)}, u32[]{:S(2)}) collective-permute-start(f32[48,128]{1,0:T(8,128)S(1)} %get-tuple-element.70), channel_id=1, source_target_pairs={{0,16},{16,0},{1,17},{17,1},{2,18},{18,2},{3,19},{19,3},{4,20},{20... | collective-permute-start | bytes 73736 | tf_op jit(solution)/shard_map/ppermute | solution.py:475
  34.1 1.3 %collective-permute-start.13 = (f32[16,128]{1,0:T(8,128)S(1)}, f32[16,128]{1,0:T(8,128)S(1)}, u32[]{:S(2)}, u32[]{:S(2)}) collective-permute-start(f32[16,128]{1,0:T(8,128)S(1)} %slice.7), channel_id=1, source_target_pairs={{0,4},{4,0},{8,12},{12,8},{1,5},{5,1},{9,13},{13,9},{2,6},{6,2},{1... | collective-permute-start | bytes 24584 | tf_op jit(solution)/shard_map/ppermute | solution.py:477
  35.4 0.4 %shard_map.82 = (f32[576,128]{1,0:T(8,128)S(1)}, f32[288,128]{1,0:T(8,128)S(1)}) custom-call(f32[576,128]{1,0:T(8,128)S(1)} %get-tuple-element.60.u_ref, f32[288,128]{1,0:T(8,128)S(1)} %get-tuple-element.43.t_ref, f32[288,128]{1,0:T(8,128)S(1)} %get-tuple-element.44.tv_ref, f32[288,128]{1,0:T(8,128)S(1)} %get-tuple-element.45.tw_ref, ...), custom_call_target="tpu_custom_call" | custom-call | tf_op jit(solution)/shard_map/pallas_call | solution.py:20
  35.8 0.4 %collective-permute-done.13.refs_5_ = f32[16,128]{1,0:T(8,128)S(1)} collective-permute-done((f32[16,128]{1,0:T(8,128)S(1)}, f32[16,128]{1,0:T(8,128)S(1)}, u32[]{:S(2)}, u32[]{:S(2)}) %collective-permute-start.13) | collective-permute-done | bytes 8224 | tf_op jit(solution)/shard_map/ppermute | solution.py:477
  36.2 0.2 collective-permute-done.14.refs_6_
  36.5 0.0 collective-permute-done.12.refs_4_
  36.5 0.9 %shard_map.83 = f32[576,128]{1,0:T(8,128)} custom-call(f32[576,128]{1,0:T(8,128)S(1)} %get-tuple-element.67.refs_0_, f32[288,128]{1,0:T(8,128)S(1)} %get-tuple-element.68.refs_1_, s32[288,128]{1,0:T(8,128)S(1)} %bitcast.15, f32[1440,128]{1,0:T(8,128)S(1)} %bitcast.9, f32[64,128]{1,0:T(8,128)S(1)} %collective-permute-done.12.refs_4_, ...), custom_call_target="tpu_custom_call" | custom-call | tf_op jit(solution)/shard_map/pallas_call | solution.py:20
  (4 shorter events, 0.0 us)
Async XLA Ops:
  1.2 7.4 %collective-permute-start = (f32[39,4,128]{2,1,0:T(4,128)S(1)}, f32[39,4,128]{2,1,0:T(4,128)S(1)}, u32[]{:S(2)}, u32[]{:S(2)}) collective-permute-start(f32[39,4,128]{2,1,0:T(4,128)S(1)} %get-tuple-element.39), channel_id=1, source_target_pairs={{0,1},{1,0},{2,3},{3,2},{4,5},{5,4},{6,7},{7,6},{8,9},{9,8},{10,11... | collective-permute-start | bytes 239624 | tf_op jit(solution)/shard_map/ppermute | solution.py:425
  4.3 9.0 %collective-permute-start.1 = (f32[39,4,128]{2,1,0:T(4,128)S(1)}, f32[39,4,128]{2,1,0:T(4,128)S(1)}, u32[]{:S(2)}, u32[]{:S(2)}) collective-permute-start(f32[39,4,128]{2,1,0:T(4,128)S(1)} %get-tuple-element.40), channel_id=1, source_target_pairs={{0,2},{1,3},{2,0},{3,1},{4,6},{5,7},{6,4},{7,5},{8,10},{9,11},{10,... | collective-permute-start | bytes 239624 | tf_op jit(solution)/shard_map/ppermute | solution.py:425
  6.9 6.5 %collective-permute-start.2 = (f32[39,4,128]{2,1,0:T(4,128)S(1)}, f32[39,4,128]{2,1,0:T(4,128)S(1)}, u32[]{:S(2)}, u32[]{:S(2)}) collective-permute-start(f32[39,4,128]{2,1,0:T(4,128)S(1)} %get-tuple-element.41), channel_id=1, source_target_pairs={{0,3},{1,2},{2,1},{3,0},{4,7},{5,6},{6,5},{7,4},{8,11},{9,10},{10,... | collective-permute-start | bytes 239624 | tf_op jit(solution)/shard_map/ppermute | solution.py:425
  6.9 0.7 %copy-start.2 = (s32[128]{0:T(128)S(1)}, s32[128]{0:T(128)}, u32[]{:S(2)}) copy-start(s32[128]{0:T(128)} %param.13) | copy-start | bytes 1540
  7.5 10.0 %copy-start.1 = (s32[18,16,128]{2,1,0:T(8,128)S(1)}, s32[18,16,128]{2,1,0:T(8,128)}, u32[]{:S(2)}) copy-start(s32[18,16,128]{2,1,0:T(8,128)} %param.9) | copy-start | bytes 442372
  8.6 13.1 %copy-start = (f32[5,18,16,128]{3,2,1,0:T(8,128)S(1)}, f32[5,18,16,128]{3,2,1,0:T(8,128)}, u32[]{:S(2)}) copy-start(f32[5,18,16,128]{3,2,1,0:T(8,128)} %param.8) | copy-start | bytes 2211844
  13.6 4.7 %collective-permute-start.4 = (f32[32,128]{1,0:T(8,128)S(1)}, f32[32,128]{1,0:T(8,128)S(1)}, u32[]{:S(2)}, u32[]{:S(2)}) collective-permute-start(f32[32,128]{1,0:T(8,128)S(1)} %get-tuple-element.48), channel_id=1, source_target_pairs={{0,2},{1,3},{2,0},{3,1},{4,6},{5,7},{6,4},{7,5},{8,10},{9,11},{10,... | collective-permute-start | bytes 49160 | tf_op jit(solution)/shard_map/ppermute | solution.py:425
  16.1 5.5 %collective-permute-start.5 = (f32[32,128]{1,0:T(8,128)S(1)}, f32[32,128]{1,0:T(8,128)S(1)}, u32[]{:S(2)}, u32[]{:S(2)}) collective-permute-start(f32[32,128]{1,0:T(8,128)S(1)} %get-tuple-element.48), channel_id=1, source_target_pairs={{0,3},{1,2},{2,1},{3,0},{4,7},{5,6},{6,5},{7,4},{8,11},{9,10},{10,... | collective-permute-start | bytes 49160 | tf_op jit(solution)/shard_map/ppermute | solution.py:425
  17.5 4.2 %collective-permute-start.3 = (f32[32,128]{1,0:T(8,128)S(1)}, f32[32,128]{1,0:T(8,128)S(1)}, u32[]{:S(2)}, u32[]{:S(2)}) collective-permute-start(f32[32,128]{1,0:T(8,128)S(1)} %get-tuple-element.47), channel_id=1, source_target_pairs={{0,1},{1,0},{2,3},{3,2},{4,5},{5,4},{6,7},{7,6},{8,9},{9,8},{10,11... | collective-permute-start | bytes 49160 | tf_op jit(solution)/shard_map/ppermute | solution.py:425
  21.8 4.0 %collective-permute-start.6 = (f32[64,128]{1,0:T(8,128)S(1)}, f32[64,128]{1,0:T(8,128)S(1)}, u32[]{:S(2)}, u32[]{:S(2)}) collective-permute-start(f32[64,128]{1,0:T(8,128)S(1)} %get-tuple-element.55), channel_id=1, source_target_pairs={{0,12},{4,8},{8,4},{12,0},{1,13},{5,9},{9,5},{13,1},{2,14},{6,10},... | collective-permute-start | bytes 98312 | tf_op jit(solution)/shard_map/ppermute | solution.py:476
  21.9 3.9 %collective-permute-start.8 = (f32[48,128]{1,0:T(8,128)S(1)}, f32[48,128]{1,0:T(8,128)S(1)}, u32[]{:S(2)}, u32[]{:S(2)}) collective-permute-start(f32[48,128]{1,0:T(8,128)S(1)} %get-tuple-element.56), channel_id=1, source_target_pairs={{0,16},{16,0},{1,17},{17,1},{2,18},{18,2},{3,19},{19,3},{4,20},{20... | collective-permute-start | bytes 73736 | tf_op jit(solution)/shard_map/ppermute | solution.py:475
  23.4 2.1 %collective-permute-start.7 = (f32[16,128]{1,0:T(8,128)S(1)}, f32[16,128]{1,0:T(8,128)S(1)}, u32[]{:S(2)}, u32[]{:S(2)}) collective-permute-start(f32[16,128]{1,0:T(8,128)S(1)} %slice.6), channel_id=1, source_target_pairs={{0,4},{4,0},{8,12},{12,8},{1,5},{5,1},{9,13},{13,9},{2,6},{6,2},{1... | collective-permute-start | bytes 24584 | tf_op jit(solution)/shard_map/ppermute | solution.py:477
  26.0 4.7 %collective-permute-start.10 = (f32[32,128]{1,0:T(8,128)S(1)}, f32[32,128]{1,0:T(8,128)S(1)}, u32[]{:S(2)}, u32[]{:S(2)}) collective-permute-start(f32[32,128]{1,0:T(8,128)S(1)} %get-tuple-element.63), channel_id=1, source_target_pairs={{0,2},{1,3},{2,0},{3,1},{4,6},{5,7},{6,4},{7,5},{8,10},{9,11},{10,... | collective-permute-start | bytes 49160 | tf_op jit(solution)/shard_map/ppermute | solution.py:425
  26.8 5.5 %collective-permute-start.11 = (f32[32,128]{1,0:T(8,128)S(1)}, f32[32,128]{1,0:T(8,128)S(1)}, u32[]{:S(2)}, u32[]{:S(2)}) collective-permute-start(f32[32,128]{1,0:T(8,128)S(1)} %get-tuple-element.63), channel_id=1, source_target_pairs={{0,3},{1,2},{2,1},{3,0},{4,7},{5,6},{6,5},{7,4},{8,11},{9,10},{10,... | collective-permute-start | bytes 49160 | tf_op jit(solution)/shard_map/ppermute | solution.py:425
  28.2 4.2 %collective-permute-start.9 = (f32[32,128]{1,0:T(8,128)S(1)}, f32[32,128]{1,0:T(8,128)S(1)}, u32[]{:S(2)}, u32[]{:S(2)}) collective-permute-start(f32[32,128]{1,0:T(8,128)S(1)} %get-tuple-element.62), channel_id=1, source_target_pairs={{0,1},{1,0},{2,3},{3,2},{4,5},{5,4},{6,7},{7,6},{8,9},{9,8},{10,11... | collective-permute-start | bytes 49160 | tf_op jit(solution)/shard_map/ppermute | solution.py:425
  32.5 4.0 %collective-permute-start.12 = (f32[64,128]{1,0:T(8,128)S(1)}, f32[64,128]{1,0:T(8,128)S(1)}, u32[]{:S(2)}, u32[]{:S(2)}) collective-permute-start(f32[64,128]{1,0:T(8,128)S(1)} %get-tuple-element.69), channel_id=1, source_target_pairs={{0,12},{4,8},{8,4},{12,0},{1,13},{5,9},{9,5},{13,1},{2,14},{6,10},... | collective-permute-start | bytes 98312 | tf_op jit(solution)/shard_map/ppermute | solution.py:476
  32.6 3.9 %collective-permute-start.14 = (f32[48,128]{1,0:T(8,128)S(1)}, f32[48,128]{1,0:T(8,128)S(1)}, u32[]{:S(2)}, u32[]{:S(2)}) collective-permute-start(f32[48,128]{1,0:T(8,128)S(1)} %get-tuple-element.70), channel_id=1, source_target_pairs={{0,16},{16,0},{1,17},{17,1},{2,18},{18,2},{3,19},{19,3},{4,20},{20... | collective-permute-start | bytes 73736 | tf_op jit(solution)/shard_map/ppermute | solution.py:475
  34.1 2.1 %collective-permute-start.13 = (f32[16,128]{1,0:T(8,128)S(1)}, f32[16,128]{1,0:T(8,128)S(1)}, u32[]{:S(2)}, u32[]{:S(2)}) collective-permute-start(f32[16,128]{1,0:T(8,128)S(1)} %slice.7), channel_id=1, source_target_pairs={{0,4},{4,0},{8,12},{12,8},{1,5},{5,1},{9,13},{13,9},{2,6},{6,2},{1... | collective-permute-start | bytes 24584 | tf_op jit(solution)/shard_map/ppermute | solution.py:477
